TPU v7x, 32 devices: a whole 2x2x4 slice. The times are simulated.
32 devices in a mesh: survey: 2 (over x), sector: 16 (over z, y, core).
Axes of the slice: x: 2, y: 2, z: 4, core: 2. Of those that a mesh axis runs over, the one named last changes fastest.
Arguments:
- raw_pings: bfloat16 [32, 512, 2, 1024], P('survey', 'sector'), parts along dimension 0, may hold values from -6 to 6
- focus_matrix: bfloat16 [2, 2048, 512], replicated, may hold values from -0.25 to 0.25
- start_angle: int32 [32], P('survey'), parts along dimension 0, may hold values from 0 to 2047
- ping_count: int32 [32], P('survey'), parts along dimension 0, may hold values from 256 to 512, as said below
Outputs:
- coherence: float32 [32, 2048, 1024], P(('survey', 'sector')), parts along dimension 0
- interferogram: bfloat16 [32, 2, 2048, 1024], P(('survey', 'sector')), parts along dimension 0
There are 2 independent parts, one for each index of `survey`. A program takes and returns all parts, laid end to end along the dimension named above; an argument that names none is the same for every part. Nothing has to cross between parts.
Inputs may be any that keep to these rules, and one draw needn't show every extreme that they name: `ping_count`: every value lies between 256 and 512, and at least one sector holds all 512 pings.
All inputs are finite; a program needn't handle non-finite values.
Results may differ from a plain program's by a relative error of at most 0.0057.
Values may be sent and summed in bfloat16 or wider, within the bound.
No kernel may reach another device: no remote copies, remote signals or barrier semaphores. Data moves between devices by JAX's collectives and lax.ppermute only.
A program may use at most 192 MiB of HBM per device.

v0:
```python
import jax
import jax.numpy as jnp
from jax import lax
from jax.sharding import PartitionSpec as P

WIN = 9


def shifted(block, axis, distance):
    devices = range(lax.axis_size(axis))
    route = [((i - distance) % len(devices), i) for i in devices]
    return lax.ppermute(block, axis, route)


def focus_sector(raw, angle_step, valid_pings, stacked):
    pings_here = raw.shape[0]
    ranges_here = raw.shape[2]
    columns_count = stacked.shape[0] // 2
    ping_mask = (jnp.arange(pings_here, dtype=jnp.int32) < valid_pings).astype(jnp.bfloat16)
    masked = raw * ping_mask[:, None, None]
    product = jnp.dot(
        stacked, masked.reshape(pings_here, 2 * ranges_here), preferred_element_type=jnp.float32
    )
    product = product.reshape(2, columns_count, 2, ranges_here)
    real_part = product[0, :, 0] - product[1, :, 1]
    imag_part = product[0, :, 1] + product[1, :, 0]
    columns = jnp.arange(columns_count, dtype=jnp.int32)
    turn_index = angle_step * columns % columns_count
    phase_turn = 2.0 * jnp.pi / columns_count * turn_index.astype(jnp.float32)
    cosine = jnp.cos(phase_turn)[:, None]
    sine_part = jnp.sin(phase_turn)[:, None]
    mean_power = jnp.mean(real_part * real_part + imag_part * imag_part, axis=0)
    inverse_rms = lax.rsqrt(mean_power + 1e-06)
    turned_real = (real_part * cosine + imag_part * sine_part) * inverse_rms
    turned_imag = (imag_part * cosine - real_part * sine_part) * inverse_rms
    return jnp.stack([turned_real, turned_imag], axis=1).astype(jnp.bfloat16)


def window_sum(field, axis, span):
    half_span = span // 2
    length_axis = field.shape[axis]
    widths = [(0, 0)] * field.ndim
    widths[axis] = (half_span, half_span)
    padded = jnp.pad(field, widths)
    total = lax.slice_in_dim(padded, 0, length_axis, axis=axis)
    for offset in range(1, span):
        total = total + lax.slice_in_dim(padded, offset, offset + length_axis, axis=axis)
    return total


def compare(own_image, other_image, span):
    f_real = own_image[:, 0].astype(jnp.float32)
    f_imag = own_image[:, 1].astype(jnp.float32)
    g_real = other_image[:, 0].astype(jnp.float32)
    g_imag = other_image[:, 1].astype(jnp.float32)
    fields = jnp.stack(
        [
            f_real * g_real + f_imag * g_imag,
            f_imag * g_real - f_real * g_imag,
            f_real * f_real + f_imag * f_imag,
            g_real * g_real + g_imag * g_imag,
        ],
        axis=0,
    )
    looked = window_sum(window_sum(fields, 1, span), 2, span)
    magnitude = jnp.sqrt(looked[0] * looked[0] + looked[1] * looked[1])
    energy = jnp.sqrt(looked[2] * looked[3] + 1e-06)
    coherence = magnitude / energy
    interferogram = (looked[0:2] / float(span * span)).astype(jnp.bfloat16)
    return (coherence, interferogram)


def body(raw_pings, focus_matrix, start_angle, ping_count):
    stacked = focus_matrix.reshape(2 * focus_matrix.shape[1], focus_matrix.shape[2])
    position = lax.axis_index("sector")

    def prepare(pieces, sector):
        return focus_sector(pieces[0], start_angle[sector], ping_count[sector], stacked)[None]

    own_image = (lambda pieces: prepare(pieces, position))(
        lax.all_to_all(raw_pings, "sector", split_axis=0, concat_axis=1, tiled=True)
    )
    other_image = shifted(own_image, "sector", -1)
    coherence, interferogram = compare(own_image[0], other_image[0], WIN)
    return (coherence[None], interferogram[None])


def solution(mesh):
    return jax.shard_map(
        body,
        mesh=mesh,
        in_specs=(P("survey", "sector", None, None), P(), P("survey"), P("survey")),
        out_specs=(P(("survey", "sector"), None, None), P(("survey", "sector"), None, None, None)),
        check_vma=False,
    )
```

profile of v0, /device:TPU:0, one launch (start us, length us, event | category | flops | bytes accessed | tf_op | source)
XLA Modules:
  0.0 722.9 jit_solution(4973740520128592052)
XLA Ops:
  0.6 7.4 %all-to-all-start = ((bf16[16,32,2,1024]{3,2,1,0:T(2,128)(2,1)}), bf16[16,32,2,1024]{3,2,1,0:T(2,128)(2,1)S(1)}, u32[]{:S(2)}, u32[]{:S(2)}) async-start(bf16[16,32,2,1024]{3,2,1,0:T(2,128)(2,1)} %param.4), calls=%async_computation | async-start | bytes 4194304 | tf_op jit(solution)/shard_map/all_to_all | solution.py:81
  8.1 1.2 dynamic_slice.6
  9.3 1.2 dynamic_slice.7
  11.9 37.1 %all-to-all-done = bf16[16,32,2,1024]{3,2,1,0:T(2,128)(2,1)S(1)} async-done(((bf16[16,32,2,1024]{3,2,1,0:T(2,128)(2,1)}), bf16[16,32,2,1024]{3,2,1,0:T(2,128)(2,1)S(1)}, u32[]{:S(2)}, u32[]{:S(2)}) %all-to-all-start) | async-done | bytes 2097184 | tf_op jit(solution)/shard_map/all_to_all | solution.py:81
  49.0 1.9 broadcast_multiply_fusion
  51.5 17.5 %convolution_bitcast_fusion = f32[4096,2048]{0,1:T(8,128)} fusion(bf16[512,2048]{1,0:T(8,128)(2,1)S(1)} %bitcast.52, bf16[4096,512]{1,0:T(8,128)(2,1)} %bitcast.53), kind=kOutput, calls=%fused_computation.23 | convolution fusion | flops 8589934592 | bytes 39845888 | tf_op jit(solution)/shard_map/dot_general | solution.py:21
  69.0 42.6 %reshape.411 = f32[2,2048,2,1024]{1,0,3,2:T(2,128)} reshape(f32[4096,2048]{0,1:T(8,128)} %convolution_bitcast_fusion) | data formatting | bytes 67108864 | tf_op jit(solution)/shard_map/reshape | solution.py:24
  111.7 39.8 %fusion.42 = (f32[1,2048,1,1024]{1,0,3,2:T(1,128)}, f32[1,2048,1,1024]{1,0,3,2:T(1,128)}, f32[1,2048,1,1024]{1,0,3,2:T(1,128)}, f32[1,2048,1,1024]{1,0,3,2:T(1,128)}) fusion(f32[2,2048,2,1024]{1,0,3,2:T(2,128)} %reshape.411), kind=kLoop, calls=%fused_computation.80 | loop fusion | bytes 67108864 | tf_op jit(solution)/shard_map/slice | solution.py:25
  151.5 20.7 %copy.10 = f32[1,2048,1,1024]{3,1,2,0:T(8,128)} copy(f32[1,2048,1,1024]{1,0,3,2:T(1,128)} %get-tuple-element.10) | data formatting | bytes 16777216
  172.3 20.7 %copy.11 = f32[1,2048,1,1024]{3,1,2,0:T(8,128)} copy(f32[1,2048,1,1024]{1,0,3,2:T(1,128)} %get-tuple-element.8) | data formatting | bytes 16777216
  192.9 20.5 %copy.12 = f32[1,2048,1,1024]{3,1,2,0:T(8,128)} copy(f32[1,2048,1,1024]{1,0,3,2:T(1,128)} %get-tuple-element.9) | data formatting | bytes 16777216
  213.5 20.5 %copy.13 = f32[1,2048,1,1024]{3,1,2,0:T(8,128)} copy(f32[1,2048,1,1024]{1,0,3,2:T(1,128)} %get-tuple-element.11) | data formatting | bytes 16777216
  234.0 19.2 %add_reduce_fusion = (f32[1024]{0:T(1024)S(1)}, f32[1,2048,1,1024]{3,1,2,0:T(8,128)}, f32[1,2048,1,1024]{3,1,2,0:T(8,128)}) fusion(f32[1,2048,1,1024]{3,1,2,0:T(8,128)} %copy.12, f32[1,2048,1,1024]{3,1,2,0:T(8,128)} %copy.13, f32[1,2048,1,1024]{3,1,2,0:T(8,128)} %copy.10, f32[1,2048,1,1024]{3,1,2,0:T(8,128)} %copy.11), kind=kLoop, calls=%fused_computation.64 | loop fusion | flops 12581888 | bytes 50335744 | tf_op jit(solution)/shard_map/reduce_sum | solution.py:32
  253.3 8.6 %multiply_convert_fusion.1 = (bf16[1,2048,1,1024]{3,1,2,0:T(8,128)(2,1)S(1)}, bf16[1,2048,1,1024]{3,1,2,0:T(8,128)(2,1)}) fusion(f32[1,2048,1,1024]{3,1,2,0:T(8,128)} %get-tuple-element.6, f32[1,2048,1,1024]{3,1,2,0:T(8,128)} %get-tuple-element.7, f32[1024]{0:T(1024)S(1)} %add_rsqrt_fusion, f32[2048]{0:T(1024)S(1)} %get-tuple-element.17, ...), kind=kLoop, calls=%fused_computation.63 | loop fusion | flops 20971520 | bytes 25186304 | tf_op jit(solution)/shard_map/convert
  261.9 6.2 pad_maximum_fusion.1
  268.0 9.8 %collective-permute-start = (bf16[1,2048,2,1024]{3,1,2,0:T(8,128)(2,1)}, bf16[1,2048,2,1024]{3,1,2,0:T(8,128)(2,1)S(1)}, u32[]{:S(2)}, u32[]{:S(2)}) collective-permute-start(bf16[1,2048,2,1024]{3,1,2,0:T(8,128)(2,1)} %pad_maximum_fusion.1), channel_id=1, source_target_pairs={{1,0},{2,1},{3,2},{4,3},{5,4},{6,5},{7,6},{8,7},{9,8},{10,9},{11,1... | collective-permute-start | bytes 25165832 | tf_op jit(solution)/shard_map/ppermute | solution.py:12
  277.9 91.3 %collective-permute-done = bf16[1,2048,2,1024]{3,1,2,0:T(8,128)(2,1)S(1)} collective-permute-done((bf16[1,2048,2,1024]{3,1,2,0:T(8,128)(2,1)}, bf16[1,2048,2,1024]{3,1,2,0:T(8,128)(2,1)S(1)}, u32[]{:S(2)}, u32[]{:S(2)}) %collective-permute-start) | collective-permute-done | bytes 8388640 | tf_op jit(solution)/shard_map/ppermute | solution.py:12
  369.2 13.3 %fusion.14 = (f32[1,2048,1024]{2,1,0:T(8,128)}, bf16[2048,1,1024]{2,0,1:T(8,128)(2,1)S(1)}, bf16[2048,1,1024]{2,0,1:T(8,128)(2,1)}) fusion(bf16[2048,2,1024]{2,0,1:T(8,128)(2,1)S(1)} %bitcast.49, f32[1024]{0:T(1024)S(1)} %add_rsqrt_fusion, f32[2048]{0:T(1024)S(1)} %get-tuple-element.17, f32[1,2048,1,1024]{3,1,2,0:T(8,128)} %get-tuple-element.7, ...), kind=kLoop, calls=%fused_computation.37 | loop fusion | flops 35651584 | bytes 41963520 | tf_op jit(solution)/shard_map/add | solution.py:58
  382.5 11.1 %fusion.18 = (f32[1,2048,1024]{2,1,0:T(8,128)}, f32[1,2048,1024]{2,1,0:T(8,128)}, f32[1,2048,1024]{2,1,0:T(8,128)}) fusion(bf16[2048,1,1024]{2,0,1:T(8,128)(2,1)S(1)} %get-tuple-element.3, bf16[2048,1,1024]{2,0,1:T(8,128)(2,1)} %get-tuple-element.4, bf16[2048,2,1024]{2,0,1:T(8,128)(2,1)S(1)} %bitcast.50), kind=kLoop, calls=%fused_computation.41 | loop fusion | flops 27262976 | bytes 41943040 | tf_op jit(solution)/shard_map/sub | solution.py:59
  393.6 23.4 %pad_maximum_fusion = f32[4,2048,1024]{2,1,0:T(8,128)} fusion(f32[1,2048,1024]{2,1,0:T(8,128)} %get-tuple-element.15, f32[1,2048,1024]{2,1,0:T(8,128)} %get-tuple-element.16, f32[1,2048,1024]{2,1,0:T(8,128)} %get-tuple-element.14, f32[1,2048,1024]{2,1,0:T(8,128)} %get-tuple-element.2), kind=kLoop, calls=%fused_computation.16 | loop fusion | flops 25165824 | bytes 67108864 | tf_op jit(solution)/shard_map/stack | solution.py:56
  417.0 131.8 %slice_add_fusion = f32[4,2048,1024]{2,1,0:T(8,128)} fusion(f32[4,2048,1024]{2,1,0:T(8,128)} %pad_maximum_fusion), kind=kLoop, calls=%fused_computation.17 | loop fusion | flops 67108864 | bytes 67108864 | tf_op jit(solution)/shard_map/add | solution.py:47
  548.8 147.7 %fusion.7 = f32[4,2048,1024]{2,1,0:T(8,128)} fusion(f32[4,2048,1024]{2,1,0:T(8,128)} %slice_add_fusion), kind=kLoop, calls=%fused_computation.15 | loop fusion | flops 67108864 | bytes 67108864 | tf_op jit(solution)/shard_map/add | solution.py:47
  696.5 9.6 %fusion.19 = bf16[1,2,2048,1024]{3,2,1,0:T(8,128)(2,1)} fusion(f32[4,2048,1024]{2,1,0:T(8,128)} %fusion.7), kind=kLoop, calls=%fused_computation.42 | loop fusion | flops 8388608 | bytes 25165824 | tf_op jit(solution)/shard_map/broadcast_in_dim | solution.py:85
  706.1 16.7 %fusion.22 = f32[1,2048,1024]{2,1,0:T(8,128)} fusion(f32[4,2048,1024]{2,1,0:T(8,128)} %fusion.7), kind=kLoop, calls=%fused_computation.46 | loop fusion | flops 12582912 | bytes 41943040 | tf_op jit(solution)/shard_map/div | solution.py:68
  (4 shorter events, 2.0 us)
Async XLA Ops:
  0.6 48.4 %all-to-all-start = ((bf16[16,32,2,1024]{3,2,1,0:T(2,128)(2,1)}), bf16[16,32,2,1024]{3,2,1,0:T(2,128)(2,1)S(1)}, u32[]{:S(2)}, u32[]{:S(2)}) async-start(bf16[16,32,2,1024]{3,2,1,0:T(2,128)(2,1)} %param.4), calls=%async_computation | async-start | bytes 4194304 | tf_op jit(solution)/shard_map/all_to_all | solution.py:81
  268.0 101.1 %collective-permute-start = (bf16[1,2048,2,1024]{3,1,2,0:T(8,128)(2,1)}, bf16[1,2048,2,1024]{3,1,2,0:T(8,128)(2,1)S(1)}, u32[]{:S(2)}, u32[]{:S(2)}) collective-permute-start(bf16[1,2048,2,1024]{3,1,2,0:T(8,128)(2,1)} %pad_maximum_fusion.1), channel_id=1, source_target_pairs={{1,0},{2,1},{3,2},{4,3},{5,4},{6,5},{7,6},{8,7},{9,8},{10,9},{11,1... | collective-permute-start | bytes 25165832 | tf_op jit(solution)/shard_map/ppermute | solution.py:12
where the time goes:
time: 726 us; the launch traced here: 723 us
  other arithmetic  391 us (54%)
  local copies, waits for them, and re-layouts  168 us (23%)
  waiting for transfers between devices  128 us (18%)
  matrix products  17.5 us (2%)
  starting transfers between devices  17.3 us (2%)
    add x2, other arithmetic, window_sum(): total + lax.slice_in_dim(padded, offset, offset + length_axis, axis=axis)  280 us
    ppermute x1, waiting for transfers between devices, shifted(): return lax.ppermute(block, axis, route)  91.3 us
    unnamed x5, local copies, waits for them, and re-layouts  83.1 us
    reshape x1, local copies, waits for them, and re-layouts, focus_sector(): product = product.reshape(2, columns_count, 2, ranges_here)  42.6 us
    slice x1, local copies, waits for them, and re-layouts, focus_sector(): real_part = product[0, :, 0] - product[1, :, 1]  39.8 us
    all_to_all x1, waiting for transfers between devices, body(): lax.all_to_all(raw_pings, 'sector', split_axis=0, concat_axis=1, tiled=True)  37.1 us
    another operation x1, other arithmetic, compare(): jnp.stack([f_real * g_real + f_imag * g_imag, f_imag * g_real - f_real *...  23.4 us
    reduce_sum x1, other arithmetic, focus_sector(): mean_power = jnp.mean(real_part * real_part + imag_part * imag_part, axis=0)  19.2 us
  transfers between devices with their start and end apart: 2, of which 2 were waited for; matrix products, arithmetic and copies ran while one was open for 1% of the time, Pallas kernels for 0%

commit v1 on v0

--- a/solution.py
+++ b/solution.py
@@ -2,6 +2,7 @@
 import jax.numpy as jnp
 from jax import lax
 from jax.sharding import PartitionSpec as P
+from jax.lax import all_to_all, axis_size
 
 WIN = 9
 
@@ -78,7 +79,9 @@
         return focus_sector(pieces[0], start_angle[sector], ping_count[sector], stacked)[None]
 
     own_image = (lambda pieces: prepare(pieces, position))(
-        lax.all_to_all(raw_pings, "sector", split_axis=0, concat_axis=1, tiled=True)
+        jnp.concatenate(
+            all_to_all(jnp.stack(jnp.split(raw_pings, axis_size("sector"), 0)), "sector", 0, 0), 1
+        )
     )
     other_image = shifted(own_image, "sector", -1)
     coherence, interferogram = compare(own_image[0], other_image[0], WIN)

time: 726 us -> 753 us (1.037)
  local copies, waits for them, and re-layouts: 168 us -> 193 us
    unnamed x5 -> x24, local copies, waits for them, and re-layouts: 83.1 us -> 108 us
  transfers between devices with their start and end apart: 2 -> 2, of which waited for: 2 -> 2; matrix products, arithmetic and copies ran while one was open for 1% -> 0% of each run, Pallas kernels for 0% -> 0%
where the time goes in v1:
time: 753 us; the launch traced here: 749 us
  other arithmetic  391 us (52%)
  local copies, waits for them, and re-layouts  193 us (26%)
  waiting for transfers between devices  130 us (17%)
  matrix products  17.5 us (2%)
  starting transfers between devices  17.2 us (2%)
    add x2, other arithmetic, window_sum(): total + lax.slice_in_dim(padded, offset, offset + length_axis, axis=axis)  279 us
    unnamed x24, local copies, waits for them, and re-layouts  108 us
    ppermute x1, waiting for transfers between devices, shifted(): return lax.ppermute(block, axis, route)  91.3 us
    reshape x1, local copies, waits for them, and re-layouts, focus_sector(): product = product.reshape(2, columns_count, 2, ranges_here)  42.6 us
    slice x1, local copies, waits for them, and re-layouts, focus_sector(): real_part = product[0, :, 0] - product[1, :, 1]  39.8 us
    all_to_all x1, waiting for transfers between devices, body(): all_to_all(jnp.stack(jnp.split(raw_pings, axis_size('sector'), 0)), 'sect...  38.3 us
    another operation x1, other arithmetic, compare(): jnp.stack([f_real * g_real + f_imag * g_imag, f_imag * g_real - f_real *...  23.4 us
    reduce_sum x1, other arithmetic, focus_sector(): mean_power = jnp.mean(real_part * real_part + imag_part * imag_part, axis=0)  19.2 us
  transfers between devices with their start and end apart: 2, of which 2 were waited for; matrix products, arithmetic and copies ran while one was open for 0% of the time, Pallas kernels for 0%

profile of v1, /device:TPU:0, one launch (start us, length us, event | category | flops | bytes accessed | tf_op | source)
XLA Modules:
  0.0 749.1 jit_solution(8647365512729383399)
XLA Ops:
  0.6 1.7 bitcast_dynamic-update-slice_fusion.15
  2.3 1.6 bitcast_dynamic-update-slice_fusion.14
  27.1 7.4 all-to-all-start
  37.1 38.3 %all-to-all-done = bf16[16,1,32,2,1024]{4,3,2,1,0:T(2,128)(2,1)S(1)} async-done(((bf16[16,1,32,2,1024]{4,3,2,1,0:T(2,128)(2,1)}), bf16[16,1,32,2,1024]{4,3,2,1,0:T(2,128)(2,1)S(1)}, u32[]{:S(2)}, u32[]{:S(2)}) %all-to-all-start) | async-done | bytes 2097184 | tf_op jit(solution)/shard_map/all_to_all | solution.py:83
  75.5 1.9 broadcast_multiply_fusion
  78.0 17.5 %convolution_bitcast_fusion = f32[4096,2048]{0,1:T(8,128)} fusion(bf16[512,2048]{1,0:T(8,128)(2,1)S(1)} %bitcast.84, bf16[4096,512]{1,0:T(8,128)(2,1)} %bitcast.85), kind=kOutput, calls=%fused_computation.23 | convolution fusion | flops 8589934592 | bytes 39845888 | tf_op jit(solution)/shard_map/dot_general | solution.py:22
  95.5 42.6 %reshape.406 = f32[2,2048,2,1024]{1,0,3,2:T(2,128)} reshape(f32[4096,2048]{0,1:T(8,128)} %convolution_bitcast_fusion) | data formatting | bytes 67108864 | tf_op jit(solution)/shard_map/reshape | solution.py:25
  138.1 39.8 %fusion.42 = (f32[1,2048,1,1024]{1,0,3,2:T(1,128)}, f32[1,2048,1,1024]{1,0,3,2:T(1,128)}, f32[1,2048,1,1024]{1,0,3,2:T(1,128)}, f32[1,2048,1,1024]{1,0,3,2:T(1,128)}) fusion(f32[2,2048,2,1024]{1,0,3,2:T(2,128)} %reshape.406), kind=kLoop, calls=%fused_computation.96 | loop fusion | bytes 67108864 | tf_op jit(solution)/shard_map/slice | solution.py:26
  177.9 20.7 %copy.10 = f32[1,2048,1,1024]{3,1,2,0:T(8,128)} copy(f32[1,2048,1,1024]{1,0,3,2:T(1,128)} %get-tuple-element.10) | data formatting | bytes 16777216
  198.6 20.7 %copy.11 = f32[1,2048,1,1024]{3,1,2,0:T(8,128)} copy(f32[1,2048,1,1024]{1,0,3,2:T(1,128)} %get-tuple-element.8) | data formatting | bytes 16777216
  219.3 20.5 %copy.12 = f32[1,2048,1,1024]{3,1,2,0:T(8,128)} copy(f32[1,2048,1,1024]{1,0,3,2:T(1,128)} %get-tuple-element.9) | data formatting | bytes 16777216
  239.8 20.5 %copy.13 = f32[1,2048,1,1024]{3,1,2,0:T(8,128)} copy(f32[1,2048,1,1024]{1,0,3,2:T(1,128)} %get-tuple-element.11) | data formatting | bytes 16777216
  260.4 19.2 %add_reduce_fusion = (f32[1024]{0:T(1024)S(1)}, f32[1,2048,1,1024]{3,1,2,0:T(8,128)}, f32[1,2048,1,1024]{3,1,2,0:T(8,128)}) fusion(f32[1,2048,1,1024]{3,1,2,0:T(8,128)} %copy.12, f32[1,2048,1,1024]{3,1,2,0:T(8,128)} %copy.13, f32[1,2048,1,1024]{3,1,2,0:T(8,128)} %copy.10, f32[1,2048,1,1024]{3,1,2,0:T(8,128)} %copy.11), kind=kLoop, calls=%fused_computation.64 | loop fusion | flops 12581888 | bytes 50335744 | tf_op jit(solution)/shard_map/reduce_sum | solution.py:33
  279.6 8.6 %multiply_convert_fusion.1 = (bf16[1,2048,1,1024]{3,1,2,0:T(8,128)(2,1)S(1)}, bf16[1,2048,1,1024]{3,1,2,0:T(8,128)(2,1)}) fusion(f32[1,2048,1,1024]{3,1,2,0:T(8,128)} %get-tuple-element.6, f32[1,2048,1,1024]{3,1,2,0:T(8,128)} %get-tuple-element.7, f32[1024]{0:T(1024)S(1)} %add_rsqrt_fusion, f32[2048]{0:T(1024)S(1)} %get-tuple-element.17, ...), kind=kLoop, calls=%fused_computation.63 | loop fusion | flops 20971520 | bytes 25186304 | tf_op jit(solution)/shard_map/convert
  288.2 6.2 pad_maximum_fusion.1
  294.4 9.8 %collective-permute-start = (bf16[1,2048,2,1024]{3,1,2,0:T(8,128)(2,1)}, bf16[1,2048,2,1024]{3,1,2,0:T(8,128)(2,1)S(1)}, u32[]{:S(2)}, u32[]{:S(2)}) collective-permute-start(bf16[1,2048,2,1024]{3,1,2,0:T(8,128)(2,1)} %pad_maximum_fusion.1), channel_id=1, source_target_pairs={{1,0},{2,1},{3,2},{4,3},{5,4},{6,5},{7,6},{8,7},{9,8},{10,9},{11,1... | collective-permute-start | bytes 25165832 | tf_op jit(solution)/shard_map/ppermute | solution.py:13
  304.3 91.3 %collective-permute-done = bf16[1,2048,2,1024]{3,1,2,0:T(8,128)(2,1)S(1)} collective-permute-done((bf16[1,2048,2,1024]{3,1,2,0:T(8,128)(2,1)}, bf16[1,2048,2,1024]{3,1,2,0:T(8,128)(2,1)S(1)}, u32[]{:S(2)}, u32[]{:S(2)}) %collective-permute-start) | collective-permute-done | bytes 8388640 | tf_op jit(solution)/shard_map/ppermute | solution.py:13
  395.5 13.3 %fusion.14 = (f32[1,2048,1024]{2,1,0:T(8,128)}, bf16[2048,1,1024]{2,0,1:T(8,128)(2,1)S(1)}, bf16[2048,1,1024]{2,0,1:T(8,128)(2,1)}) fusion(bf16[2048,2,1024]{2,0,1:T(8,128)(2,1)S(1)} %bitcast.81, f32[1024]{0:T(1024)S(1)} %add_rsqrt_fusion, f32[2048]{0:T(1024)S(1)} %get-tuple-element.17, f32[1,2048,1,1024]{3,1,2,0:T(8,128)} %get-tuple-element.7, ...), kind=kLoop, calls=%fused_computation.37 | loop fusion | flops 35651584 | bytes 41963520 | tf_op jit(solution)/shard_map/add | solution.py:59
  408.8 11.1 %fusion.18 = (f32[1,2048,1024]{2,1,0:T(8,128)}, f32[1,2048,1024]{2,1,0:T(8,128)}, f32[1,2048,1024]{2,1,0:T(8,128)}) fusion(bf16[2048,1,1024]{2,0,1:T(8,128)(2,1)S(1)} %get-tuple-element.3, bf16[2048,1,1024]{2,0,1:T(8,128)(2,1)} %get-tuple-element.4, bf16[2048,2,1024]{2,0,1:T(8,128)(2,1)S(1)} %bitcast.82), kind=kLoop, calls=%fused_computation.41 | loop fusion | flops 27262976 | bytes 41943040 | tf_op jit(solution)/shard_map/sub | solution.py:60
  420.0 23.4 %pad_maximum_fusion = f32[4,2048,1024]{2,1,0:T(8,128)} fusion(f32[1,2048,1024]{2,1,0:T(8,128)} %get-tuple-element.15, f32[1,2048,1024]{2,1,0:T(8,128)} %get-tuple-element.16, f32[1,2048,1024]{2,1,0:T(8,128)} %get-tuple-element.14, f32[1,2048,1024]{2,1,0:T(8,128)} %get-tuple-element.2), kind=kLoop, calls=%fused_computation.16 | loop fusion | flops 25165824 | bytes 67108864 | tf_op jit(solution)/shard_map/stack | solution.py:57
  443.4 131.7 %slice_add_fusion = f32[4,2048,1024]{2,1,0:T(8,128)} fusion(f32[4,2048,1024]{2,1,0:T(8,128)} %pad_maximum_fusion), kind=kLoop, calls=%fused_computation.17 | loop fusion | flops 67108864 | bytes 67108864 | tf_op jit(solution)/shard_map/add | solution.py:48
  575.1 147.6 %fusion.7 = f32[4,2048,1024]{2,1,0:T(8,128)} fusion(f32[4,2048,1024]{2,1,0:T(8,128)} %slice_add_fusion), kind=kLoop, calls=%fused_computation.15 | loop fusion | flops 67108864 | bytes 67108864 | tf_op jit(solution)/shard_map/add | solution.py:48
  722.7 9.6 %fusion.19 = bf16[1,2,2048,1024]{3,2,1,0:T(8,128)(2,1)} fusion(f32[4,2048,1024]{2,1,0:T(8,128)} %fusion.7), kind=kLoop, calls=%fused_computation.42 | loop fusion | flops 8388608 | bytes 25165824 | tf_op jit(solution)/shard_map/broadcast_in_dim | solution.py:88
  732.3 16.7 %fusion.22 = f32[1,2048,1024]{2,1,0:T(8,128)} fusion(f32[4,2048,1024]{2,1,0:T(8,128)} %fusion.7), kind=kLoop, calls=%fused_computation.46 | loop fusion | flops 12582912 | bytes 41943040 | tf_op jit(solution)/shard_map/div | solution.py:69
  (24 shorter events, 26.3 us)
Async XLA Ops:
  0.6 33.9 %copy-start = (s32[16]{0:T(128)S(1)}, s32[16]{0:T(128)}, u32[]{:S(2)}) copy-start(s32[16]{0:T(128)} %param.7) | copy-start | bytes 196
  0.6 34.4 %copy-start.1 = (s32[16]{0:T(128)S(1)}, s32[16]{0:T(128)}, u32[]{:S(2)}) copy-start(s32[16]{0:T(128)} %param.6) | copy-start | bytes 196
  27.1 48.4 %all-to-all-start = ((bf16[16,1,32,2,1024]{4,3,2,1,0:T(2,128)(2,1)}), bf16[16,1,32,2,1024]{4,3,2,1,0:T(2,128)(2,1)S(1)}, u32[]{:S(2)}, u32[]{:S(2)}) async-start(bf16[16,1,32,2,1024]{4,3,2,1,0:T(2,128)(2,1)} %bitcast_dynamic-update-slice_fusion), calls=%async_computation | async-start | bytes 4194304 | tf_op jit(solution)/shard_map/all_to_all | solution.py:83
  294.4 101.1 %collective-permute-start = (bf16[1,2048,2,1024]{3,1,2,0:T(8,128)(2,1)}, bf16[1,2048,2,1024]{3,1,2,0:T(8,128)(2,1)S(1)}, u32[]{:S(2)}, u32[]{:S(2)}) collective-permute-start(bf16[1,2048,2,1024]{3,1,2,0:T(8,128)(2,1)} %pad_maximum_fusion.1), channel_id=1, source_target_pairs={{1,0},{2,1},{3,2},{4,3},{5,4},{6,5},{7,6},{8,7},{9,8},{10,9},{11,1... | collective-permute-start | bytes 25165832 | tf_op jit(solution)/shard_map/ppermute | solution.py:13
